TPU v7x, 128 devices: a whole 4x4x4 slice. The times are simulated.
128 devices in a mesh: seq: 8 (over z, core), exp: 16 (over y, x).
Axes of the slice: x: 4, y: 4, z: 4, core: 2. Of those that a mesh axis runs over, the one named last changes fastest.
Arguments:
- attn_query: bfloat16 [2048, 6144], P('seq', 'exp'), may hold values from -6 to 6
- attn_key: bfloat16 [2048, 6144], P('seq', 'exp'), may hold values from -6 to 6
- attn_value: bfloat16 [2048, 6144], P('seq', 'exp'), may hold values from -40 to 40
- log_decay: float32 [48, 2048], P('exp', 'seq'), may hold values from -1.5 to 0
- residual: bfloat16 [2048, 6144], P('seq', 'exp'), may hold values from -6 to 6
- norm_gain: bfloat16 [6144], P('exp'), may hold values from 0.099609375 to 1.8984375
- expert_ids: int32 [2048, 2], P('seq'), may hold values from 0 to 15, as said below
- router_weight: bfloat16 [6144, 16], P(None, 'seq'), may hold values from -0.078125 to 0.078125
- gate_weight: bfloat16 [16, 6144, 4608], P('seq', None, 'exp'), may hold values from -0.078125 to 0.078125
- up_weight: bfloat16 [16, 6144, 4608], P('seq', None, 'exp'), may hold values from -0.078125 to 0.078125
- down_weight: bfloat16 [16, 4608, 6144], P('seq', 'exp'), may hold values from -0.125 to 0.125
Outputs:
- layer_out: bfloat16 [2048, 6144], P('seq', 'exp')
Inputs may be any that keep to these rules, and one draw needn't show every extreme that they name: `expert_ids`: each row names two different experts. In every section of 256 consecutive rows no expert is named more than 64 times, and in every section some experts are named exactly 64 times.
All inputs are finite; a program needn't handle non-finite values.
Results may differ from a plain program's by a relative error of at most 0.017.
Values may be sent and summed in bfloat16 or wider, within the bound.
A program may use at most 192 MiB of HBM per device.

v0:
```python
import jax
import jax.numpy as jnp
from jax import lax
from jax.sharding import PartitionSpec as P


def shifted(array, axis, by):
    count = lax.axis_size(axis)
    pairs = [(i, i + by) for i in range(count) if 0 <= i + by < count]
    return lax.ppermute(array, axis, pairs)


def on_device(
    attn_query,
    attn_key,
    attn_value,
    log_decay,
    residual,
    norm_gain,
    expert_ids,
    router_weight,
    gate_weight,
    up_weight,
    down_weight,
):
    heads_here = log_decay.shape[0]
    length = log_decay.shape[1]
    head_size = attn_query.shape[1] // heads_here
    query_rows = attn_query.reshape(length, heads_here, head_size)
    key_rows = attn_key.reshape(length, heads_here, head_size)
    value_rows = attn_value.reshape(length, heads_here, head_size)
    cumulative = jnp.cumsum(log_decay, axis=1)
    causal = lax.broadcasted_iota(jnp.int32, (length, length), 0) >= lax.broadcasted_iota(
        jnp.int32, (length, length), 1
    )
    decay_gap = jnp.where(causal[None], cumulative[:, :, None] - cumulative[:, None, :], 0.0)
    decay_mask = jnp.where(causal[None], jnp.exp(decay_gap), 0.0)
    scores = jnp.einsum("thd,shd->hts", query_rows, key_rows, preferred_element_type=jnp.float32)
    weights = (scores * decay_mask).astype(jnp.bfloat16)
    intra_part = jnp.einsum("hts,shd->thd", weights, value_rows, preferred_element_type=jnp.float32)
    key_fade = jnp.exp(cumulative[:, -1:] - cumulative)
    scaled = (key_fade.T[:, :, None] * key_rows.astype(jnp.float32)).astype(jnp.bfloat16)
    local_state = jnp.einsum("shd,she->hde", scaled, value_rows, preferred_element_type=jnp.float32)
    section_fade = jnp.exp(cumulative[:, -1])
    incoming = jnp.zeros_like(local_state)
    for repeat_index in range(lax.axis_size("seq") - 1):
        incoming = shifted(section_fade[:, None, None] * incoming + local_state, "seq", 1)
    inter_part = jnp.einsum(
        "thd,hde->the", query_rows.astype(jnp.float32), incoming, precision=lax.Precision.HIGHEST
    )
    attn_out = intra_part + jnp.exp(cumulative).T[:, :, None] * inter_part
    mean_square = jnp.mean(attn_out * attn_out, axis=2, keepdims=True)
    normed = (attn_out / jnp.sqrt(mean_square + 1e-06)).reshape(length, heads_here * head_size)
    stream = (residual.astype(jnp.float32) + norm_gain.astype(jnp.float32) * normed).astype(
        jnp.bfloat16
    )
    experts_here = router_weight.shape[1]
    groups = lax.axis_size("seq")
    expert_count = experts_here * groups
    capacity = 4 * length // expert_count
    features = stream.shape[1]
    choices_per_token = expert_ids.shape[1]
    flat_ids = expert_ids.reshape(-1)
    expert_iota = lax.broadcasted_iota(jnp.int32, (1, expert_count), 1)
    onehot = (flat_ids[:, None] == expert_iota).astype(jnp.int32)
    running = jnp.cumsum(onehot, axis=0)
    slot_index = jnp.sum(running * onehot, axis=1) - 1
    target = flat_ids * capacity + slot_index
    place_iota = lax.broadcasted_iota(jnp.int32, (expert_count * capacity, 1), 0)
    route_matrix = (
        (place_iota == target[None, :])
        .astype(jnp.bfloat16)
        .reshape(expert_count * capacity, length, choices_per_token)
        .sum(axis=2)
    )
    outgoing = jnp.dot(route_matrix, stream, preferred_element_type=jnp.float32).astype(
        jnp.bfloat16
    )
    outgoing = outgoing.reshape(groups, experts_here, capacity, features)
    portion = lax.all_gather(
        lax.all_to_all(outgoing, "seq", split_axis=0, concat_axis=0, tiled=True),
        "exp",
        axis=3,
        tiled=True,
    )
    gate_acc = jnp.einsum(
        "sjcd,jdf->sjcf", portion, gate_weight, preferred_element_type=jnp.float32
    )
    upward = jnp.einsum("sjcd,jdf->sjcf", portion, up_weight, preferred_element_type=jnp.float32)
    logits = jnp.einsum("sjcd,dj->sjc", portion, router_weight, preferred_element_type=jnp.float32)
    hidden_act = (jax.nn.silu(gate_acc) * upward).astype(jnp.bfloat16)
    expert_out = lax.psum_scatter(
        jnp.einsum(
            "sjcf,jfd->dsjc", hidden_act, down_weight, preferred_element_type=jnp.float32
        ).astype(jnp.bfloat16),
        "exp",
        scatter_dimension=0,
        tiled=True,
    ).astype(jnp.float32)
    routed = (jax.nn.sigmoid(logits)[None] * expert_out).astype(jnp.bfloat16)
    returned = lax.all_to_all(routed, "seq", split_axis=1, concat_axis=1, tiled=True)
    returned = returned.reshape(features, expert_count * capacity)
    combined = lax.dot_general(
        route_matrix, returned, (((0,), (1,)), ((), ())), preferred_element_type=jnp.float32
    )
    return (stream.astype(jnp.float32) + combined).astype(jnp.bfloat16)


def solution(mesh):
    in_specs = (
        P("seq", "exp"),
        P("seq", "exp"),
        P("seq", "exp"),
        P("exp", "seq"),
        P("seq", "exp"),
        P("exp"),
        P("seq", None),
        P(None, "seq"),
        P("seq", None, "exp"),
        P("seq", None, "exp"),
        P("seq", "exp", None),
    )
    out_specs = P("seq", "exp")
    return jax.shard_map(
        on_device, mesh=mesh, in_specs=in_specs, out_specs=out_specs, check_vma=False
    )
```

profile of v0, /device:TPU:1, one launch (start us, length us, event | category | flops | bytes accessed | tf_op | source)
XLA Modules:
  0.0 400.8 jit_solution(6427846024970069958)
XLA Ops:
  7.3 0.9 reduce-window.14
  8.8 1.1 copy.80
  9.9 1.1 copy.85
  11.2 4.9 %collective-permute-start = (f32[3,128,128]{2,1,0:T(8,128)S(1)}, f32[3,128,128]{2,1,0:T(8,128)S(1)}, u32[]{:S(2)}, u32[]{:S(2)}) collective-permute-start(f32[3,128,128]{2,1,0:T(8,128)S(1)} %get-tuple-element.9), channel_id=1, source_target_pairs={{0,16},{16,32},{32,48},{48,64},{64,80},{80,96},{96,112},{1,17},{17... | collective-permute-start | bytes 589832 | tf_op jit(solution)/shard_map/ppermute | solution.py:10
  18.8 4.4 %collective-permute-start.1 = (f32[3,128,128]{2,1,0:T(8,128)S(1)}, f32[3,128,128]{2,1,0:T(8,128)S(1)}, u32[]{:S(2)}, u32[]{:S(2)}) collective-permute-start(f32[3,128,128]{2,1,0:T(8,128)S(1)} %multiply_add_fusion.5), channel_id=1, source_target_pairs={{0,16},{16,32},{32,48},{48,64},{64,80},{80,96},{96,112},{1,17},{17... | collective-permute-start | bytes 589832 | tf_op jit(solution)/shard_map/ppermute | solution.py:10
  23.2 1.2 reduce-window.16
  24.4 1.4 collective-permute-done.1
  25.9 4.4 %collective-permute-start.2 = (f32[3,128,128]{2,1,0:T(8,128)S(1)}, f32[3,128,128]{2,1,0:T(8,128)S(1)}, u32[]{:S(2)}, u32[]{:S(2)}) collective-permute-start(f32[3,128,128]{2,1,0:T(8,128)S(1)} %multiply_add_fusion.4), channel_id=1, source_target_pairs={{0,16},{16,32},{32,48},{48,64},{64,80},{80,96},{96,112},{1,17},{17... | collective-permute-start | bytes 589832 | tf_op jit(solution)/shard_map/ppermute | solution.py:10
  30.7 2.2 collective-permute-done.2
  33.0 4.4 %collective-permute-start.3 = (f32[3,128,128]{2,1,0:T(8,128)S(1)}, f32[3,128,128]{2,1,0:T(8,128)S(1)}, u32[]{:S(2)}, u32[]{:S(2)}) collective-permute-start(f32[3,128,128]{2,1,0:T(8,128)S(1)} %multiply_add_fusion.3), channel_id=1, source_target_pairs={{0,16},{16,32},{32,48},{48,64},{64,80},{80,96},{96,112},{1,17},{17... | collective-permute-start | bytes 589832 | tf_op jit(solution)/shard_map/ppermute | solution.py:10
  37.6 1.1 copy.79
  38.7 1.3 collective-permute-done.3
  40.1 4.4 %collective-permute-start.4 = (f32[3,128,128]{2,1,0:T(8,128)S(1)}, f32[3,128,128]{2,1,0:T(8,128)S(1)}, u32[]{:S(2)}, u32[]{:S(2)}) collective-permute-start(f32[3,128,128]{2,1,0:T(8,128)S(1)} %multiply_add_fusion.2), channel_id=1, source_target_pairs={{0,16},{16,32},{32,48},{48,64},{64,80},{80,96},{96,112},{1,17},{17... | collective-permute-start | bytes 589832 | tf_op jit(solution)/shard_map/ppermute | solution.py:10
  45.2 1.9 collective-permute-done.4
  47.1 4.4 %collective-permute-start.5 = (f32[3,128,128]{2,1,0:T(8,128)S(1)}, f32[3,128,128]{2,1,0:T(8,128)S(1)}, u32[]{:S(2)}, u32[]{:S(2)}) collective-permute-start(f32[3,128,128]{2,1,0:T(8,128)S(1)} %multiply_add_fusion.1), channel_id=1, source_target_pairs={{0,16},{16,32},{32,48},{48,64},{64,80},{80,96},{96,112},{1,17},{17... | collective-permute-start | bytes 589832 | tf_op jit(solution)/shard_map/ppermute | solution.py:10
  52.0 2.1 collective-permute-done.5
  54.2 4.4 %collective-permute-start.6 = (f32[3,128,128]{2,1,0:T(8,128)S(1)}, f32[3,128,128]{2,1,0:T(8,128)S(1)}, u32[]{:S(2)}, u32[]{:S(2)}) collective-permute-start(f32[3,128,128]{2,1,0:T(8,128)S(1)} %multiply_add_fusion), channel_id=1, source_target_pairs={{0,16},{16,32},{32,48},{48,64},{64,80},{80,96},{96,112},{1,17},{17... | collective-permute-start | bytes 589832 | tf_op jit(solution)/shard_map/ppermute | solution.py:10
  59.1 2.1 collective-permute-done.6
  62.4 18.3 %all_to_all.10 = bf16[8,2,64,384]{3,2,1,0:T(8,128)(2,1)S(1)} all-to-all(bf16[8,2,64,384]{3,2,1,0:T(8,128)(2,1)S(1)} %bitcast.110), channel_id=1, replica_groups=mesh['seq'=8,'exp'=16] {'seq'}, dimensions={0} | all-to-all | bytes 1572864 | tf_op jit(solution)/shard_map/all_to_all | solution.py:81
  80.6 1.0 copy.95
  81.9 98.5 %all-gather.2.cloned.1.call-done = bf16[8,2,64,6144]{3,2,0,1:T(8,128)(2,1)} async-done(((bf16[8,2,64,384]{3,2,0,1:T(8,128)(2,1)}), bf16[8,2,64,6144]{3,2,0,1:T(8,128)(2,1)}) %all-gather.2.cloned.1.call-update) | async-done | bytes 12582928 | tf_op jit(solution)/shard_map/all_gather | solution.py:80
  180.3 11.8 %fusion.3 = f32[2,8,64,288]{3,2,1,0:T(8,128)S(1)} fusion(bf16[8,2,64,6144]{3,2,0,1:T(8,128)(2,1)} %all-gather.2.cloned.1.call-done, bf16[2,6144,288]{1,2,0:T(8,128)(2,1)} %param.19), kind=kOutput, calls=%fused_computation.4 | convolution fusion | flops 3623878656 | bytes 20840448 | tf_op jit(solution)/shard_map/sjcd,jdf->sjcf/dot_general | solution.py:86
  192.1 8.9 %fusion.6 = bf16[8,2,64,288]{3,2,0,1:T(8,128)(2,1)S(1)} fusion(f32[2,8,64,288]{3,2,1,0:T(8,128)S(1)} %fusion.3, bf16[8,2,64,6144]{3,2,0,1:T(8,128)(2,1)S(1)} %copy-done.1, bf16[2,6144,288]{1,2,0:T(8,128)(2,1)} %param.20), kind=kOutput, calls=%fused_computation.9 | convolution fusion | flops 3625648128 | bytes 21430272 | tf_op jit(solution)/shard_map/sjcd,jdf->sjcf/dot_general | solution.py:89
  201.1 12.6 %convert_bitcast_fusion = bf16[6144,8,2,64]{0,3,1,2:T(8,128)(2,1)} fusion(bf16[8,2,64,288]{3,2,0,1:T(8,128)(2,1)S(1)} %fusion.6, bf16[2,288,6144]{2,1,0:T(8,128)(2,1)} %param.21), kind=kOutput, calls=%fused_computation | convolution fusion | flops 3630170112 | bytes 20250624 | tf_op jit(solution)/shard_map/sjcf,jfd->dsjc/dot_general | solution.py:93
  213.7 29.7 %copy.107 = bf16[6144,8,2,64]{3,1,2,0:T(8,128)(2,1)} copy(bf16[6144,8,2,64]{0,3,1,2:T(8,128)(2,1)} %convert_bitcast_fusion) | data formatting | bytes 25165824
  243.4 33.4 %reshape.128 = bf16[6144,1024]{1,0:T(8,128)(2,1)} reshape(bf16[6144,2,8,64]{3,2,1,0:T(8,128)(2,1)} %bitcast.108) | data formatting | bytes 25165824
  276.8 7.9 %fusion.29 = f32[2,1,8,64]{3,1,2,0:T(1,128)S(1)} fusion(bf16[8,2,64,6144]{3,2,0,1:T(8,128)(2,1)} %all-gather.2.cloned.1.call-done, bf16[6144,2,1,1]{0,1,2,3:T(2,128)(2,1)S(1)} %bitcast.107), kind=kOutput, calls=%fused_computation.49 | convolution fusion | flops 12582912 | bytes 12611584 | tf_op jit(solution)/shard_map/sjcd,dj->sjc/dot_general | solution.py:90
  284.7 86.8 %reduce-scatter.4.cloned.1.call-done = bf16[384,1024]{1,0:T(8,128)(2,1)} async-done(((bf16[6144,1024]{1,0:T(8,128)(2,1)}), bf16[384,1024]{1,0:T(8,128)(2,1)}) %reduce-scatter.4.cloned.1.call-update) | async-done | bytes 786448
  371.5 2.5 reshape.129
  374.0 1.2 copy.108
  375.5 17.3 %all_to_all.11 = bf16[384,8,2,64]{0,3,2,1:T(8,128)(2,1)S(1)} all-to-all(bf16[384,8,2,64]{0,3,2,1:T(8,128)(2,1)S(1)} %copy.96), channel_id=1, replica_groups=mesh['seq'=8,'exp'=16] {'seq'}, dimensions={1} | all-to-all | bytes 1572864 | tf_op jit(solution)/shard_map/all_to_all | solution.py:101
  392.8 1.1 fusion.17
  (55 shorter events, 8.6 us)
Async XLA Ops:
  6.5 270.3 %copy-start = (bf16[6144,2]{0,1:T(2,128)(2,1)S(1)}, bf16[6144,2]{0,1:T(2,128)(2,1)}, u32[]{:S(2)}) copy-start(bf16[6144,2]{0,1:T(2,128)(2,1)} %param.18) | copy-start | bytes 73732
  6.5 55.3 %copy-start.2 = (bf16[256,384]{1,0:T(8,128)(2,1)S(1)}, bf16[256,384]{1,0:T(8,128)(2,1)}, u32[]{:S(2)}) copy-start(bf16[256,384]{1,0:T(8,128)(2,1)} %param.15) | copy-start | bytes 589828
  6.5 173.8 %all-gather.2.cloned.1.call-start = ((), (), s32[]{:S(2)}) async-start(), calls=%async_computation.3 | async-start | bytes 13369344 | tf_op jit(solution)/shard_map/all_gather | solution.py:80
  11.2 7.5 %collective-permute-start = (f32[3,128,128]{2,1,0:T(8,128)S(1)}, f32[3,128,128]{2,1,0:T(8,128)S(1)}, u32[]{:S(2)}, u32[]{:S(2)}) collective-permute-start(f32[3,128,128]{2,1,0:T(8,128)S(1)} %get-tuple-element.9), channel_id=1, source_target_pairs={{0,16},{16,32},{32,48},{48,64},{64,80},{80,96},{96,112},{1,17},{17... | collective-permute-start | bytes 589832 | tf_op jit(solution)/shard_map/ppermute | solution.py:10
  18.8 7.0 %collective-permute-start.1 = (f32[3,128,128]{2,1,0:T(8,128)S(1)}, f32[3,128,128]{2,1,0:T(8,128)S(1)}, u32[]{:S(2)}, u32[]{:S(2)}) collective-permute-start(f32[3,128,128]{2,1,0:T(8,128)S(1)} %multiply_add_fusion.5), channel_id=1, source_target_pairs={{0,16},{16,32},{32,48},{48,64},{64,80},{80,96},{96,112},{1,17},{17... | collective-permute-start | bytes 589832 | tf_op jit(solution)/shard_map/ppermute | solution.py:10
  25.9 7.0 %collective-permute-start.2 = (f32[3,128,128]{2,1,0:T(8,128)S(1)}, f32[3,128,128]{2,1,0:T(8,128)S(1)}, u32[]{:S(2)}, u32[]{:S(2)}) collective-permute-start(f32[3,128,128]{2,1,0:T(8,128)S(1)} %multiply_add_fusion.4), channel_id=1, source_target_pairs={{0,16},{16,32},{32,48},{48,64},{64,80},{80,96},{96,112},{1,17},{17... | collective-permute-start | bytes 589832 | tf_op jit(solution)/shard_map/ppermute | solution.py:10
  33.0 7.0 %collective-permute-start.3 = (f32[3,128,128]{2,1,0:T(8,128)S(1)}, f32[3,128,128]{2,1,0:T(8,128)S(1)}, u32[]{:S(2)}, u32[]{:S(2)}) collective-permute-start(f32[3,128,128]{2,1,0:T(8,128)S(1)} %multiply_add_fusion.3), channel_id=1, source_target_pairs={{0,16},{16,32},{32,48},{48,64},{64,80},{80,96},{96,112},{1,17},{17... | collective-permute-start | bytes 589832 | tf_op jit(solution)/shard_map/ppermute | solution.py:10
  40.1 7.0 %collective-permute-start.4 = (f32[3,128,128]{2,1,0:T(8,128)S(1)}, f32[3,128,128]{2,1,0:T(8,128)S(1)}, u32[]{:S(2)}, u32[]{:S(2)}) collective-permute-start(f32[3,128,128]{2,1,0:T(8,128)S(1)} %multiply_add_fusion.2), channel_id=1, source_target_pairs={{0,16},{16,32},{32,48},{48,64},{64,80},{80,96},{96,112},{1,17},{17... | collective-permute-start | bytes 589832 | tf_op jit(solution)/shard_map/ppermute | solution.py:10
  47.1 7.0 %collective-permute-start.5 = (f32[3,128,128]{2,1,0:T(8,128)S(1)}, f32[3,128,128]{2,1,0:T(8,128)S(1)}, u32[]{:S(2)}, u32[]{:S(2)}) collective-permute-start(f32[3,128,128]{2,1,0:T(8,128)S(1)} %multiply_add_fusion.1), channel_id=1, source_target_pairs={{0,16},{16,32},{32,48},{48,64},{64,80},{80,96},{96,112},{1,17},{17... | collective-permute-start | bytes 589832 | tf_op jit(solution)/shard_map/ppermute | solution.py:10
  54.2 7.0 %collective-permute-start.6 = (f32[3,128,128]{2,1,0:T(8,128)S(1)}, f32[3,128,128]{2,1,0:T(8,128)S(1)}, u32[]{:S(2)}, u32[]{:S(2)}) collective-permute-start(f32[3,128,128]{2,1,0:T(8,128)S(1)} %multiply_add_fusion), channel_id=1, source_target_pairs={{0,16},{16,32},{32,48},{48,64},{64,80},{80,96},{96,112},{1,17},{17... | collective-permute-start | bytes 589832 | tf_op jit(solution)/shard_map/ppermute | solution.py:10
  81.6 289.9 %reduce-scatter.4.cloned.1.call-start = ((), (), s32[]{:S(2)}) async-start(), calls=%async_computation.4 | async-start | bytes 13369344
  180.3 11.8 %copy-start.1 = (bf16[8,2,64,6144]{3,2,0,1:T(8,128)(2,1)S(1)}, bf16[8,2,64,6144]{3,2,0,1:T(8,128)(2,1)}, u32[]{:S(2)}) copy-start(bf16[8,2,64,6144]{3,2,0,1:T(8,128)(2,1)} %all-gather.2.cloned.1.call-done) | copy-start | bytes 37748740
Sparse Core Ops, SparseCore 0:
  81.7 98.5 all-gather.1
  276.9 94.5 reduce-scatter.3
where the time goes:
time: 403 us; the launch traced here: 401 us
  waiting for transfers between devices  197 us (49%)
  local copies, waits for them, and re-layouts  73.9 us (18%)
  matrix products  43.9 us (11%)
  blocking collectives  35.6 us (9%)
  starting transfers between devices  31.5 us (8%)
  between operations  13.7 us (3%)
  other arithmetic  5.1 us (1%)
    all_gather x1, waiting for transfers between devices, on_device(): lax.all_gather(lax.all_to_all(outgoing, 'seq', split_axis=0, concat_axis=...  98.5 us
    unnamed x3, waiting for transfers between devices  86.8 us
    unnamed x16, local copies, waits for them, and re-layouts  70.9 us
    ppermute x7, starting transfers between devices, shifted(): return lax.ppermute(array, axis, pairs)  31.3 us
    all_to_all x1, blocking collectives, on_device(): lax.all_to_all(outgoing, 'seq', split_axis=0, concat_axis=0, tiled=True)  18.3 us
    all_to_all x1, blocking collectives, on_device(): lax.all_to_all(routed, 'seq', split_axis=1, concat_axis=1, tiled=True)  17.3 us
    dot_general x1, matrix products, on_device(): jnp.einsum('sjcf,jfd->dsjc', hidden_act, down_weight, preferred_element_t...  12.6 us
    dot_general x1, matrix products, on_device(): jnp.einsum('sjcd,jdf->sjcf', portion, gate_weight, preferred_element_type...  11.8 us
  transfers between devices with their start and end apart: 9, of which 9 were waited for; matrix products, arithmetic and copies ran while one was open for 4% of the time, Pallas kernels for 0%

commit v1 on v0

--- a/solution.py
+++ b/solution.py
@@ -77,12 +77,24 @@
         jnp.bfloat16
     )
     outgoing = outgoing.reshape(groups, experts_here, capacity, features)
-    portion = lax.all_gather(
-        lax.all_to_all(outgoing, "seq", split_axis=0, concat_axis=0, tiled=True),
-        "exp",
-        axis=3,
-        tiled=True,
-    )
+    x = lax.all_to_all(outgoing, "seq", split_axis=0, concat_axis=0, tiled=True)
+    size, mine, span = (lax.axis_size("exp"), lax.axis_index("exp"), x.shape[3])
+    right = [(i_2, (i_2 + 1) % size) for i_2 in range(size)]
+    left = [(i_2, (i_2 - 1) % size) for i_2 in range(size)]
+    portion = jnp.zeros((*x.shape[:3], size * span, *x.shape[3 + 1 :]), x.dtype)
+    portion = lax.dynamic_update_slice_in_dim(portion, x, mine * span, axis=3)
+    from_left = from_right = x
+    middle = size // 2
+    for step in range(1, middle + 1):
+        from_left = lax.ppermute(from_left, "exp", right)
+        portion = lax.dynamic_update_slice_in_dim(
+            portion, from_left, (mine - step) % size * span, axis=3
+        )
+        if step < size - middle:
+            from_right = lax.ppermute(from_right, "exp", left)
+            portion = lax.dynamic_update_slice_in_dim(
+                portion, from_right, (mine + step) % size * span, axis=3
+            )
     gate_acc = jnp.einsum(
         "sjcd,jdf->sjcf", portion, gate_weight, preferred_element_type=jnp.float32
     )

time: 403 us -> 457 us (1.13)
  starting transfers between devices: 31.5 us -> 67.2 us
  local copies, waits for them, and re-layouts: 73.9 us -> 98.2 us
  waiting for transfers between devices: 197 us -> 190 us
    all_gather x1 -> x0, waiting for transfers between devices: 98.5 us -> none  [on_device(): lax.all_gather(lax.all_to_all(outgoing, 'seq', split_axis=0, concat_axis=...]
    ppermute x0 -> x15, waiting for transfers between devices: none -> 87.4 us  [the longest x8 70.5 us: on_device(): from_left = lax.ppermute(from_left, 'exp', right)]
    ppermute x0 -> x15, starting transfers between devices: none -> 36 us  [the longest x7 34.7 us: on_device(): from_right = lax.ppermute(from_right, 'exp', left)]
    dynamic_update_slice x0 -> x16, local copies, waits for them, and re-layouts: none -> 19.1 us  [the longest x8 9.53 us: on_device(): lax.dynamic_update_slice_in_dim(portion, from_left, (mine - step) % size...]
    broadcast_in_dim x0 -> x1, local copies, waits for them, and re-layouts: none -> 6.04 us  [on_device(): portion = jnp.zeros((*x.shape[:3], size * span, *x.shape[3 + 1:]), x.dtype)]
    unnamed x3 -> x2, waiting for transfers between devices: 86.8 us -> 91.1 us
    unnamed x16 -> x22, local copies, waits for them, and re-layouts: 70.9 us -> 71 us
  transfers between devices with their start and end apart: 9 -> 23, of which waited for: 9 -> 20; matrix products, arithmetic and copies ran while one was open for 4% -> 8% of each run, Pallas kernels for 0% -> 0%
where the time goes in v1:
time: 457 us; the launch traced here: 455 us
  waiting for transfers between devices  190 us (42%)
  local copies, waits for them, and re-layouts  98.2 us (21%)
  starting transfers between devices  67.2 us (15%)
  matrix products  44 us (10%)
  blocking collectives  35.6 us (8%)
  between operations  13.7 us (3%)
  other arithmetic  6.04 us (1%)
    unnamed x2, waiting for transfers between devices  91.1 us
    unnamed x22, local copies, waits for them, and re-layouts  71 us
    ppermute x8, waiting for transfers between devices, on_device(): from_left = lax.ppermute(from_left, 'exp', right)  70.5 us
    ppermute x7, starting transfers between devices, on_device(): from_right = lax.ppermute(from_right, 'exp', left)  34.7 us
    ppermute x7, starting transfers between devices, shifted(): return lax.ppermute(array, axis, pairs)  31.3 us
    all_to_all x1, blocking collectives, on_device(): x = lax.all_to_all(outgoing, 'seq', split_axis=0, concat_axis=0, tiled=True)  18.3 us
    all_to_all x1, blocking collectives, on_device(): lax.all_to_all(routed, 'seq', split_axis=1, concat_axis=1, tiled=True)  17.3 us
    ppermute x7, waiting for transfers between devices, on_device(): from_right = lax.ppermute(from_right, 'exp', left)  16.9 us
  transfers between devices with their start and end apart: 23, of which 20 were waited for; matrix products, arithmetic and copies ran while one was open for 8% of the time, Pallas kernels for 0%

profile of v1, /device:TPU:1, one launch (start us, length us, event | category | flops | bytes accessed | tf_op | source)
XLA Modules:
  0.0 455.0 jit_solution(15612553029655314498)
XLA Ops:
  11.2 4.9 %collective-permute-start = (f32[3,128,128]{2,1,0:T(8,128)S(1)}, f32[3,128,128]{2,1,0:T(8,128)S(1)}, u32[]{:S(2)}, u32[]{:S(2)}) collective-permute-start(f32[3,128,128]{2,1,0:T(8,128)S(1)} %get-tuple-element.9), channel_id=1, source_target_pairs={{0,16},{16,32},{32,48},{48,64},{64,80},{80,96},{96,112},{1,17},{17... | collective-permute-start | bytes 589832 | tf_op jit(solution)/shard_map/ppermute | solution.py:10
  18.8 4.4 collective-permute-start.1
  25.9 4.4 collective-permute-start.2
  33.0 4.4 collective-permute-start.3
  40.0 4.4 collective-permute-start.4
  47.1 4.4 collective-permute-start.5
  54.2 4.4 collective-permute-start.6
  63.2 18.3 %all_to_all.10 = bf16[8,2,64,384]{3,2,1,0:T(8,128)(2,1)S(1)} all-to-all(bf16[8,2,64,384]{3,2,1,0:T(8,128)(2,1)S(1)} %bitcast.110), channel_id=1, replica_groups=mesh['seq'=8,'exp'=16] {'seq'}, dimensions={0} | all-to-all | bytes 1572864 | tf_op jit(solution)/shard_map/all_to_all | solution.py:80
  86.5 16.7 %collective-permute-done.7 = bf16[8,2,64,384]{3,2,1,0:T(8,128)(2,1)S(1)} collective-permute-done((bf16[8,2,64,384]{3,2,1,0:T(8,128)(2,1)S(1)}, bf16[8,2,64,384]{3,2,1,0:T(8,128)(2,1)S(1)}, u32[]{:S(2)}, u32[]{:S(2)}) %collective-permute-start.7) | collective-permute-done | bytes 786464 | tf_op jit(solution)/shard_map/ppermute | solution.py:89
  103.2 4.8 %collective-permute-start.10 = (bf16[8,2,64,384]{3,2,1,0:T(8,128)(2,1)S(1)}, bf16[8,2,64,384]{3,2,1,0:T(8,128)(2,1)}, u32[]{:S(2)}, u32[]{:S(2)}) collective-permute-start(bf16[8,2,64,384]{3,2,1,0:T(8,128)(2,1)S(1)} %collective-permute-done.8), channel_id=1, source_target_pairs={{0,15},{1,0},{2,1},{3,2},{4,3},{5,4},{6,5},{7,6},{8,7},{9,8},{10,9... | collective-permute-start | bytes 2359304 | tf_op jit(solution)/shard_map/ppermute | solution.py:94
  107.9 15.9 %collective-permute-done.9 = bf16[8,2,64,384]{3,2,1,0:T(8,128)(2,1)} collective-permute-done((bf16[8,2,64,384]{3,2,1,0:T(8,128)(2,1)S(1)}, bf16[8,2,64,384]{3,2,1,0:T(8,128)(2,1)}, u32[]{:S(2)}, u32[]{:S(2)}) %collective-permute-start.9) | collective-permute-done | bytes 786464 | tf_op jit(solution)/shard_map/ppermute | solution.py:89
  123.8 4.8 %collective-permute-start.12 = (bf16[8,2,64,384]{3,2,1,0:T(8,128)(2,1)}, bf16[8,2,64,384]{3,2,1,0:T(8,128)(2,1)S(1)}, u32[]{:S(2)}, u32[]{:S(2)}) collective-permute-start(bf16[8,2,64,384]{3,2,1,0:T(8,128)(2,1)} %collective-permute-done.10), channel_id=1, source_target_pairs={{0,15},{1,0},{2,1},{3,2},{4,3},{5,4},{6,5},{7,6},{8,7},{9,8},{10,9... | collective-permute-start | bytes 2359304 | tf_op jit(solution)/shard_map/ppermute | solution.py:94
  128.6 15.0 %collective-permute-done.11 = bf16[8,2,64,384]{3,2,1,0:T(8,128)(2,1)S(1)} collective-permute-done((bf16[8,2,64,384]{3,2,1,0:T(8,128)(2,1)}, bf16[8,2,64,384]{3,2,1,0:T(8,128)(2,1)S(1)}, u32[]{:S(2)}, u32[]{:S(2)}) %collective-permute-start.11) | collective-permute-done | bytes 786464 | tf_op jit(solution)/shard_map/ppermute | solution.py:89
  143.7 6.0 %broadcast_in_dim.25 = bf16[8,2,64,6144]{3,2,0,1:T(8,128)(2,1)} broadcast(bf16[]{:T(256)} %constant.114.clone.1), dimensions={} | broadcast | bytes 12582914 | tf_op jit(solution)/shard_map/broadcast_in_dim | solution.py:84
  151.8 4.9 %collective-permute-start.14 = (bf16[8,2,64,384]{3,2,1,0:T(8,128)(2,1)S(1)}, bf16[8,2,64,384]{3,2,1,0:T(8,128)(2,1)S(1)}, u32[]{:S(2)}, u32[]{:S(2)}) collective-permute-start(bf16[8,2,64,384]{3,2,1,0:T(8,128)(2,1)S(1)} %collective-permute-done.12), channel_id=1, source_target_pairs={{0,15},{1,0},{2,1},{3,2},{4,3},{5,4},{6,5},{7,6},{8,7},{9,8},{10,9... | collective-permute-start | bytes 2359304 | tf_op jit(solution)/shard_map/ppermute | solution.py:94
  157.8 4.6 %collective-permute-done.13 = bf16[8,2,64,384]{3,2,1,0:T(8,128)(2,1)S(1)} collective-permute-done((bf16[8,2,64,384]{3,2,1,0:T(8,128)(2,1)S(1)}, bf16[8,2,64,384]{3,2,1,0:T(8,128)(2,1)S(1)}, u32[]{:S(2)}, u32[]{:S(2)}) %collective-permute-start.13) | collective-permute-done | bytes 786464 | tf_op jit(solution)/shard_map/ppermute | solution.py:89
  169.6 5.5 %collective-permute-start.16 = (bf16[8,2,64,384]{3,2,1,0:T(8,128)(2,1)S(1)}, bf16[8,2,64,384]{3,2,1,0:T(8,128)(2,1)S(1)}, u32[]{:S(2)}, u32[]{:S(2)}) collective-permute-start(bf16[8,2,64,384]{3,2,1,0:T(8,128)(2,1)S(1)} %collective-permute-done.14), channel_id=1, source_target_pairs={{0,15},{1,0},{2,1},{3,2},{4,3},{5,4},{6,5},{7,6},{8,7},{9,8},{10,9... | collective-permute-start | bytes 2359304 | tf_op jit(solution)/shard_map/ppermute | solution.py:94
  176.2 4.0 collective-permute-done.15
  182.2 4.9 %collective-permute-done.16 = bf16[8,2,64,384]{3,2,1,0:T(8,128)(2,1)S(1)} collective-permute-done((bf16[8,2,64,384]{3,2,1,0:T(8,128)(2,1)S(1)}, bf16[8,2,64,384]{3,2,1,0:T(8,128)(2,1)S(1)}, u32[]{:S(2)}, u32[]{:S(2)}) %collective-permute-start.16) | collective-permute-done | bytes 786464 | tf_op jit(solution)/shard_map/ppermute | solution.py:94
  187.1 5.5 %collective-permute-start.18 = (bf16[8,2,64,384]{3,2,1,0:T(8,128)(2,1)S(1)}, bf16[8,2,64,384]{3,2,1,0:T(8,128)(2,1)S(1)}, u32[]{:S(2)}, u32[]{:S(2)}) collective-permute-start(bf16[8,2,64,384]{3,2,1,0:T(8,128)(2,1)S(1)} %collective-permute-done.16), channel_id=1, source_target_pairs={{0,15},{1,0},{2,1},{3,2},{4,3},{5,4},{6,5},{7,6},{8,7},{9,8},{10,9... | collective-permute-start | bytes 2359304 | tf_op jit(solution)/shard_map/ppermute | solution.py:94
  199.1 4.6 %collective-permute-done.18 = bf16[8,2,64,384]{3,2,1,0:T(8,128)(2,1)S(1)} collective-permute-done((bf16[8,2,64,384]{3,2,1,0:T(8,128)(2,1)S(1)}, bf16[8,2,64,384]{3,2,1,0:T(8,128)(2,1)S(1)}, u32[]{:S(2)}, u32[]{:S(2)}) %collective-permute-start.18) | collective-permute-done | bytes 786464 | tf_op jit(solution)/shard_map/ppermute | solution.py:94
  203.7 5.5 %collective-permute-start.20 = (bf16[8,2,64,384]{3,2,1,0:T(8,128)(2,1)S(1)}, bf16[8,2,64,384]{3,2,1,0:T(8,128)(2,1)S(1)}, u32[]{:S(2)}, u32[]{:S(2)}) collective-permute-start(bf16[8,2,64,384]{3,2,1,0:T(8,128)(2,1)S(1)} %collective-permute-done.18), channel_id=1, source_target_pairs={{0,15},{1,0},{2,1},{3,2},{4,3},{5,4},{6,5},{7,6},{8,7},{9,8},{10,9... | collective-permute-start | bytes 2359304 | tf_op jit(solution)/shard_map/ppermute | solution.py:94
  215.1 4.6 %collective-permute-done.20 = bf16[8,2,64,384]{3,2,1,0:T(8,128)(2,1)S(1)} collective-permute-done((bf16[8,2,64,384]{3,2,1,0:T(8,128)(2,1)S(1)}, bf16[8,2,64,384]{3,2,1,0:T(8,128)(2,1)S(1)}, u32[]{:S(2)}, u32[]{:S(2)}) %collective-permute-start.20) | collective-permute-done | bytes 786464 | tf_op jit(solution)/shard_map/ppermute | solution.py:94
  220.7 8.2 %collective-permute-done.21 = bf16[8,2,64,384]{3,2,1,0:T(8,128)(2,1)S(1)} collective-permute-done((bf16[8,2,64,384]{3,2,1,0:T(8,128)(2,1)S(1)}, bf16[8,2,64,384]{3,2,1,0:T(8,128)(2,1)S(1)}, u32[]{:S(2)}, u32[]{:S(2)}) %collective-permute-start.21) | collective-permute-done | bytes 786464 | tf_op jit(solution)/shard_map/ppermute | solution.py:89
  230.1 11.8 %fusion.3 = f32[2,8,64,288]{3,2,1,0:T(8,128)S(1)} fusion(bf16[8,2,64,6144]{3,2,0,1:T(8,128)(2,1)} %copy_dynamic-update-slice_fusion, bf16[2,6144,288]{1,2,0:T(8,128)(2,1)} %param.19), kind=kOutput, calls=%fused_computation.4 | convolution fusion | flops 3623878656 | bytes 20840448 | tf_op jit(solution)/shard_map/sjcd,jdf->sjcf/dot_general | solution.py:98
  241.9 8.9 %fusion.6 = bf16[8,2,64,288]{3,2,0,1:T(8,128)(2,1)S(1)} fusion(f32[2,8,64,288]{3,2,1,0:T(8,128)S(1)} %fusion.3, bf16[8,2,64,6144]{3,2,0,1:T(8,128)(2,1)S(1)} %copy-done.1, bf16[2,6144,288]{1,2,0:T(8,128)(2,1)} %param.20), kind=kOutput, calls=%fused_computation.9 | convolution fusion | flops 3625648128 | bytes 21430272 | tf_op jit(solution)/shard_map/sjcd,jdf->sjcf/dot_general | solution.py:101
  250.8 12.6 %convert_bitcast_fusion = bf16[6144,8,2,64]{0,3,1,2:T(8,128)(2,1)} fusion(bf16[8,2,64,288]{3,2,0,1:T(8,128)(2,1)S(1)} %fusion.6, bf16[2,288,6144]{2,1,0:T(8,128)(2,1)} %param.21), kind=kOutput, calls=%fused_computation | convolution fusion | flops 3630170112 | bytes 20250624 | tf_op jit(solution)/shard_map/sjcf,jfd->dsjc/dot_general | solution.py:105
  263.4 29.8 %copy.152 = bf16[6144,8,2,64]{3,1,2,0:T(8,128)(2,1)} copy(bf16[6144,8,2,64]{0,3,1,2:T(8,128)(2,1)} %convert_bitcast_fusion) | data formatting | bytes 25165824
  293.2 33.5 %reshape.128 = bf16[6144,1024]{1,0:T(8,128)(2,1)} reshape(bf16[6144,2,8,64]{3,2,1,0:T(8,128)(2,1)} %bitcast.108) | data formatting | bytes 25165824
  326.7 7.9 %fusion.29 = f32[2,1,8,64]{3,1,2,0:T(1,128)S(1)} fusion(bf16[8,2,64,6144]{3,2,0,1:T(8,128)(2,1)} %copy_dynamic-update-slice_fusion, bf16[6144,2,1,1]{0,1,2,3:T(2,128)(2,1)S(1)} %bitcast.107), kind=kOutput, calls=%fused_computation.65 | convolution fusion | flops 12582912 | bytes 12611584 | tf_op jit(solution)/shard_map/sjcd,dj->sjc/dot_general | solution.py:102
  334.6 91.1 %reduce-scatter.4.cloned.1.call-done = bf16[384,1024]{1,0:T(8,128)(2,1)} async-done(((bf16[6144,1024]{1,0:T(8,128)(2,1)}), bf16[384,1024]{1,0:T(8,128)(2,1)}) %reduce-scatter.4.cloned.1.call-update) | async-done | bytes 786448
  429.7 17.3 %all_to_all.11 = bf16[384,8,2,64]{0,3,2,1:T(8,128)(2,1)S(1)} all-to-all(bf16[384,8,2,64]{0,3,2,1:T(8,128)(2,1)S(1)} %copy.141), channel_id=1, replica_groups=mesh['seq'=8,'exp'=16] {'seq'}, dimensions={1} | all-to-all | bytes 1572864 | tf_op jit(solution)/shard_map/all_to_all | solution.py:113
  (104 shorter events, 63.2 us)
Async XLA Ops:
  6.5 320.1 %copy-start = (bf16[6144,2]{0,1:T(2,128)(2,1)S(1)}, bf16[6144,2]{0,1:T(2,128)(2,1)}, u32[]{:S(2)}) copy-start(bf16[6144,2]{0,1:T(2,128)(2,1)} %param.18) | copy-start | bytes 73732
  6.5 419.2 %reduce-scatter.4.cloned.1.call-start = ((), (), s32[]{:S(2)}) async-start(), calls=%async_computation.3 | async-start | bytes 13369344
  11.2 7.5 %collective-permute-start = (f32[3,128,128]{2,1,0:T(8,128)S(1)}, f32[3,128,128]{2,1,0:T(8,128)S(1)}, u32[]{:S(2)}, u32[]{:S(2)}) collective-permute-start(f32[3,128,128]{2,1,0:T(8,128)S(1)} %get-tuple-element.9), channel_id=1, source_target_pairs={{0,16},{16,32},{32,48},{48,64},{64,80},{80,96},{96,112},{1,17},{17... | collective-permute-start | bytes 589832 | tf_op jit(solution)/shard_map/ppermute | solution.py:10
  18.8 7.0 %collective-permute-start.1 = (f32[3,128,128]{2,1,0:T(8,128)S(1)}, f32[3,128,128]{2,1,0:T(8,128)S(1)}, u32[]{:S(2)}, u32[]{:S(2)}) collective-permute-start(f32[3,128,128]{2,1,0:T(8,128)S(1)} %multiply_add_fusion.5), channel_id=1, source_target_pairs={{0,16},{16,32},{32,48},{48,64},{64,80},{80,96},{96,112},{1,17},{17... | collective-permute-start | bytes 589832 | tf_op jit(solution)/shard_map/ppermute | solution.py:10
  25.9 7.0 %collective-permute-start.2 = (f32[3,128,128]{2,1,0:T(8,128)S(1)}, f32[3,128,128]{2,1,0:T(8,128)S(1)}, u32[]{:S(2)}, u32[]{:S(2)}) collective-permute-start(f32[3,128,128]{2,1,0:T(8,128)S(1)} %multiply_add_fusion.4), channel_id=1, source_target_pairs={{0,16},{16,32},{32,48},{48,64},{64,80},{80,96},{96,112},{1,17},{17... | collective-permute-start | bytes 589832 | tf_op jit(solution)/shard_map/ppermute | solution.py:10
  33.0 7.0 %collective-permute-start.3 = (f32[3,128,128]{2,1,0:T(8,128)S(1)}, f32[3,128,128]{2,1,0:T(8,128)S(1)}, u32[]{:S(2)}, u32[]{:S(2)}) collective-permute-start(f32[3,128,128]{2,1,0:T(8,128)S(1)} %multiply_add_fusion.3), channel_id=1, source_target_pairs={{0,16},{16,32},{32,48},{48,64},{64,80},{80,96},{96,112},{1,17},{17... | collective-permute-start | bytes 589832 | tf_op jit(solution)/shard_map/ppermute | solution.py:10
  40.0 7.0 %collective-permute-start.4 = (f32[3,128,128]{2,1,0:T(8,128)S(1)}, f32[3,128,128]{2,1,0:T(8,128)S(1)}, u32[]{:S(2)}, u32[]{:S(2)}) collective-permute-start(f32[3,128,128]{2,1,0:T(8,128)S(1)} %multiply_add_fusion.2), channel_id=1, source_target_pairs={{0,16},{16,32},{32,48},{48,64},{64,80},{80,96},{96,112},{1,17},{17... | collective-permute-start | bytes 589832 | tf_op jit(solution)/shard_map/ppermute | solution.py:10
  47.1 7.0 %collective-permute-start.5 = (f32[3,128,128]{2,1,0:T(8,128)S(1)}, f32[3,128,128]{2,1,0:T(8,128)S(1)}, u32[]{:S(2)}, u32[]{:S(2)}) collective-permute-start(f32[3,128,128]{2,1,0:T(8,128)S(1)} %multiply_add_fusion.1), channel_id=1, source_target_pairs={{0,16},{16,32},{32,48},{48,64},{64,80},{80,96},{96,112},{1,17},{17... | collective-permute-start | bytes 589832 | tf_op jit(solution)/shard_map/ppermute | solution.py:10
  54.2 7.0 %collective-permute-start.6 = (f32[3,128,128]{2,1,0:T(8,128)S(1)}, f32[3,128,128]{2,1,0:T(8,128)S(1)}, u32[]{:S(2)}, u32[]{:S(2)}) collective-permute-start(f32[3,128,128]{2,1,0:T(8,128)S(1)} %multiply_add_fusion), channel_id=1, source_target_pairs={{0,16},{16,32},{32,48},{48,64},{64,80},{80,96},{96,112},{1,17},{17... | collective-permute-start | bytes 589832 | tf_op jit(solution)/shard_map/ppermute | solution.py:10
  81.5 21.6 %collective-permute-start.7 = (bf16[8,2,64,384]{3,2,1,0:T(8,128)(2,1)S(1)}, bf16[8,2,64,384]{3,2,1,0:T(8,128)(2,1)S(1)}, u32[]{:S(2)}, u32[]{:S(2)}) collective-permute-start(bf16[8,2,64,384]{3,2,1,0:T(8,128)(2,1)S(1)} %all_to_all.10), channel_id=1, source_target_pairs={{0,1},{1,2},{2,3},{3,4},{4,5},{5,6},{6,7},{7,8},{8,9},{9,10},{10,1... | collective-permute-start | bytes 2359304 | tf_op jit(solution)/shard_map/ppermute | solution.py:89
  82.7 20.4 %collective-permute-start.8 = (bf16[8,2,64,384]{3,2,1,0:T(8,128)(2,1)S(1)}, bf16[8,2,64,384]{3,2,1,0:T(8,128)(2,1)S(1)}, u32[]{:S(2)}, u32[]{:S(2)}) collective-permute-start(bf16[8,2,64,384]{3,2,1,0:T(8,128)(2,1)S(1)} %all_to_all.10), channel_id=1, source_target_pairs={{0,15},{1,0},{2,1},{3,2},{4,3},{5,4},{6,5},{7,6},{8,7},{9,8},{10,9... | collective-permute-start | bytes 2359304 | tf_op jit(solution)/shard_map/ppermute | solution.py:94
  103.2 4.8 %copy-start.4 = (bf16[8,2,64,384]{3,2,1,0:T(8,128)(2,1)}, bf16[8,2,64,384]{3,2,1,0:T(8,128)(2,1)S(1)}, u32[]{:S(2)}) copy-start(bf16[8,2,64,384]{3,2,1,0:T(8,128)(2,1)S(1)} %collective-permute-done.7) | copy-start | bytes 2359300
  103.2 20.7 %collective-permute-start.9 = (bf16[8,2,64,384]{3,2,1,0:T(8,128)(2,1)S(1)}, bf16[8,2,64,384]{3,2,1,0:T(8,128)(2,1)}, u32[]{:S(2)}, u32[]{:S(2)}) collective-permute-start(bf16[8,2,64,384]{3,2,1,0:T(8,128)(2,1)S(1)} %collective-permute-done.7), channel_id=1, source_target_pairs={{0,1},{1,2},{2,3},{3,4},{4,5},{5,6},{6,7},{7,8},{8,9},{9,10},{10,1... | collective-permute-start | bytes 2359304 | tf_op jit(solution)/shard_map/ppermute | solution.py:89
  103.2 20.7 %copy-start.2 = (bf16[8,2,64,384]{3,2,1,0:T(8,128)(2,1)}, bf16[8,2,64,384]{3,2,1,0:T(8,128)(2,1)S(1)}, u32[]{:S(2)}) copy-start(bf16[8,2,64,384]{3,2,1,0:T(8,128)(2,1)S(1)} %collective-permute-done.8) | copy-start | bytes 2359300
  103.2 20.7 %collective-permute-start.10 = (bf16[8,2,64,384]{3,2,1,0:T(8,128)(2,1)S(1)}, bf16[8,2,64,384]{3,2,1,0:T(8,128)(2,1)}, u32[]{:S(2)}, u32[]{:S(2)}) collective-permute-start(bf16[8,2,64,384]{3,2,1,0:T(8,128)(2,1)S(1)} %collective-permute-done.8), channel_id=1, source_target_pairs={{0,15},{1,0},{2,1},{3,2},{4,3},{5,4},{6,5},{7,6},{8,7},{9,8},{10,9... | collective-permute-start | bytes 2359304 | tf_op jit(solution)/shard_map/ppermute | solution.py:94
  123.8 19.8 %collective-permute-start.11 = (bf16[8,2,64,384]{3,2,1,0:T(8,128)(2,1)}, bf16[8,2,64,384]{3,2,1,0:T(8,128)(2,1)S(1)}, u32[]{:S(2)}, u32[]{:S(2)}) collective-permute-start(bf16[8,2,64,384]{3,2,1,0:T(8,128)(2,1)} %collective-permute-done.9), channel_id=1, source_target_pairs={{0,1},{1,2},{2,3},{3,4},{4,5},{5,6},{6,7},{7,8},{8,9},{9,10},{10,1... | collective-permute-start | bytes 2359304 | tf_op jit(solution)/shard_map/ppermute | solution.py:89
  123.8 28.0 %collective-permute-start.12 = (bf16[8,2,64,384]{3,2,1,0:T(8,128)(2,1)}, bf16[8,2,64,384]{3,2,1,0:T(8,128)(2,1)S(1)}, u32[]{:S(2)}, u32[]{:S(2)}) collective-permute-start(bf16[8,2,64,384]{3,2,1,0:T(8,128)(2,1)} %collective-permute-done.10), channel_id=1, source_target_pairs={{0,15},{1,0},{2,1},{3,2},{4,3},{5,4},{6,5},{7,6},{8,7},{9,8},{10,9... | collective-permute-start | bytes 2359304 | tf_op jit(solution)/shard_map/ppermute | solution.py:94
  128.6 22.2 %copy-start.5 = (bf16[8,2,64,384]{3,2,1,0:T(8,128)(2,1)S(1)}, bf16[8,2,64,384]{3,2,1,0:T(8,128)(2,1)}, u32[]{:S(2)}) copy-start(bf16[8,2,64,384]{3,2,1,0:T(8,128)(2,1)} %copy-done.4) | copy-start | bytes 2359300
  128.6 28.1 %copy-start.3 = (bf16[8,2,64,384]{3,2,1,0:T(8,128)(2,1)S(1)}, bf16[8,2,64,384]{3,2,1,0:T(8,128)(2,1)}, u32[]{:S(2)}) copy-start(bf16[8,2,64,384]{3,2,1,0:T(8,128)(2,1)} %copy-done.2) | copy-start | bytes 2359300
  143.7 18.7 %collective-permute-start.13 = (bf16[8,2,64,384]{3,2,1,0:T(8,128)(2,1)S(1)}, bf16[8,2,64,384]{3,2,1,0:T(8,128)(2,1)S(1)}, u32[]{:S(2)}, u32[]{:S(2)}) collective-permute-start(bf16[8,2,64,384]{3,2,1,0:T(8,128)(2,1)S(1)} %collective-permute-done.11), channel_id=1, source_target_pairs={{0,1},{1,2},{2,3},{3,4},{4,5},{5,6},{6,7},{7,8},{8,9},{9,10},{10,1... | collective-permute-start | bytes 2359304 | tf_op jit(solution)/shard_map/ppermute | solution.py:89
  151.8 17.8 %collective-permute-start.14 = (bf16[8,2,64,384]{3,2,1,0:T(8,128)(2,1)S(1)}, bf16[8,2,64,384]{3,2,1,0:T(8,128)(2,1)S(1)}, u32[]{:S(2)}, u32[]{:S(2)}) collective-permute-start(bf16[8,2,64,384]{3,2,1,0:T(8,128)(2,1)S(1)} %collective-permute-done.12), channel_id=1, source_target_pairs={{0,15},{1,0},{2,1},{3,2},{4,3},{5,4},{6,5},{7,6},{8,7},{9,8},{10,9... | collective-permute-start | bytes 2359304 | tf_op jit(solution)/shard_map/ppermute | solution.py:94
  162.4 17.8 %collective-permute-start.15 = (bf16[8,2,64,384]{3,2,1,0:T(8,128)(2,1)S(1)}, bf16[8,2,64,384]{3,2,1,0:T(8,128)(2,1)S(1)}, u32[]{:S(2)}, u32[]{:S(2)}) collective-permute-start(bf16[8,2,64,384]{3,2,1,0:T(8,128)(2,1)S(1)} %collective-permute-done.13), channel_id=1, source_target_pairs={{0,1},{1,2},{2,3},{3,4},{4,5},{5,6},{6,7},{7,8},{8,9},{9,10},{10,1... | collective-permute-start | bytes 2359304 | tf_op jit(solution)/shard_map/ppermute | solution.py:89
  169.6 17.5 %collective-permute-start.16 = (bf16[8,2,64,384]{3,2,1,0:T(8,128)(2,1)S(1)}, bf16[8,2,64,384]{3,2,1,0:T(8,128)(2,1)S(1)}, u32[]{:S(2)}, u32[]{:S(2)}) collective-permute-start(bf16[8,2,64,384]{3,2,1,0:T(8,128)(2,1)S(1)} %collective-permute-done.14), channel_id=1, source_target_pairs={{0,15},{1,0},{2,1},{3,2},{4,3},{5,4},{6,5},{7,6},{8,7},{9,8},{10,9... | collective-permute-start | bytes 2359304 | tf_op jit(solution)/shard_map/ppermute | solution.py:94
  180.2 16.9 %collective-permute-start.17 = (bf16[8,2,64,384]{3,2,1,0:T(8,128)(2,1)S(1)}, bf16[8,2,64,384]{3,2,1,0:T(8,128)(2,1)S(1)}, u32[]{:S(2)}, u32[]{:S(2)}) collective-permute-start(bf16[8,2,64,384]{3,2,1,0:T(8,128)(2,1)S(1)} %collective-permute-done.15), channel_id=1, source_target_pairs={{0,1},{1,2},{2,3},{3,4},{4,5},{5,6},{6,7},{7,8},{8,9},{9,10},{10,1... | collective-permute-start | bytes 2359304 | tf_op jit(solution)/shard_map/ppermute | solution.py:89
  187.1 16.6 %collective-permute-start.18 = (bf16[8,2,64,384]{3,2,1,0:T(8,128)(2,1)S(1)}, bf16[8,2,64,384]{3,2,1,0:T(8,128)(2,1)S(1)}, u32[]{:S(2)}, u32[]{:S(2)}) collective-permute-start(bf16[8,2,64,384]{3,2,1,0:T(8,128)(2,1)S(1)} %collective-permute-done.16), channel_id=1, source_target_pairs={{0,15},{1,0},{2,1},{3,2},{4,3},{5,4},{6,5},{7,6},{8,7},{9,8},{10,9... | collective-permute-start | bytes 2359304 | tf_op jit(solution)/shard_map/ppermute | solution.py:94
  197.0 15.9 %collective-permute-start.19 = (bf16[8,2,64,384]{3,2,1,0:T(8,128)(2,1)S(1)}, bf16[8,2,64,384]{3,2,1,0:T(8,128)(2,1)S(1)}, u32[]{:S(2)}, u32[]{:S(2)}) collective-permute-start(bf16[8,2,64,384]{3,2,1,0:T(8,128)(2,1)S(1)} %collective-permute-done.17), channel_id=1, source_target_pairs={{0,1},{1,2},{2,3},{3,4},{4,5},{5,6},{6,7},{7,8},{8,9},{9,10},{10,1... | collective-permute-start | bytes 2359304 | tf_op jit(solution)/shard_map/ppermute | solution.py:89
  203.7 16.0 %collective-permute-start.20 = (bf16[8,2,64,384]{3,2,1,0:T(8,128)(2,1)S(1)}, bf16[8,2,64,384]{3,2,1,0:T(8,128)(2,1)S(1)}, u32[]{:S(2)}, u32[]{:S(2)}) collective-permute-start(bf16[8,2,64,384]{3,2,1,0:T(8,128)(2,1)S(1)} %collective-permute-done.18), channel_id=1, source_target_pairs={{0,15},{1,0},{2,1},{3,2},{4,3},{5,4},{6,5},{7,6},{8,7},{9,8},{10,9... | collective-permute-start | bytes 2359304 | tf_op jit(solution)/shard_map/ppermute | solution.py:94
  213.0 16.0 %collective-permute-start.21 = (bf16[8,2,64,384]{3,2,1,0:T(8,128)(2,1)S(1)}, bf16[8,2,64,384]{3,2,1,0:T(8,128)(2,1)S(1)}, u32[]{:S(2)}, u32[]{:S(2)}) collective-permute-start(bf16[8,2,64,384]{3,2,1,0:T(8,128)(2,1)S(1)} %collective-permute-done.19), channel_id=1, source_target_pairs={{0,1},{1,2},{2,3},{3,4},{4,5},{5,6},{6,7},{7,8},{8,9},{9,10},{10,1... | collective-permute-start | bytes 2359304 | tf_op jit(solution)/shard_map/ppermute | solution.py:89
  230.1 11.8 %copy-start.1 = (bf16[8,2,64,6144]{3,2,0,1:T(8,128)(2,1)S(1)}, bf16[8,2,64,6144]{3,2,0,1:T(8,128)(2,1)}, u32[]{:S(2)}) copy-start(bf16[8,2,64,6144]{3,2,0,1:T(8,128)(2,1)} %copy_dynamic-update-slice_fusion) | copy-start | bytes 37748740
Sparse Core Ops, SparseCore 0:
  326.8 98.8 reduce-scatter.3
